TPU v7x, 32 devices: a whole 2x2x4 slice. The times are simulated.
32 devices in a mesh: row: 4 (over y, x), col: 8 (over z, core).
Axes of the slice: x: 2, y: 2, z: 4, core: 2. Of those that a mesh axis runs over, the one named last changes fastest.
Arguments:
- matrix: float32 [6, 4, 128, 128, 8, 128], P(None, 'row', None, None, 'col'), may hold values from -6 to 6
- factors: float32 [10, 512, 512], P(None, None, 'col'), as said below
- starts: int32 [10], replicated, may hold values from 0 to 2560, as said below
Outputs:
- updated: float32 [6, 4, 128, 128, 8, 128], P(None, 'row', None, None, 'col')
Inputs may be any that keep to these rules, and one draw needn't show every extreme that they name: starts[w] = starts[0] + 256 * w, and starts[0] is a multiple of 128. Each factors[w] is orthogonal.
All inputs are finite; a program needn't handle non-finite values.
Results may differ from a plain program's by a relative error of at most 0.0001.
Values sent between devices are 32-bit elements; how exact they have to be, the bound alone decides.
No kernel may reach another device: no remote copies, remote signals or barrier semaphores. Data moves between devices by JAX's collectives and lax.ppermute only.
A program may use at most 384 MiB of HBM per device.

v0:
```python
import jax
import jax.numpy as jnp
from jax import lax
from jax.sharding import PartitionSpec as P

WIN = 512
SHIFT = 256
WINS = 10


def pick_tiles(first_tile, per_device, axis_count, position, span_tiles):
    global_tiles = (
        first_tile
        + jnp.remainder(position - first_tile, axis_count)
        + jnp.arange(per_device, dtype=jnp.int32) * axis_count
    )
    tile_valid = global_tiles < first_tile + span_tiles
    return (tile_valid, jnp.where(tile_valid, global_tiles // axis_count, 0))


def band_order(first_tile, axis_count, per_device, span_tiles):
    places = jnp.arange(span_tiles, dtype=jnp.int32)
    return jnp.remainder(first_tile + places, axis_count) * per_device + places // axis_count


def slot_order(first_tile, axis_count, per_device, span_tiles):
    slot_ids = jnp.arange(axis_count * per_device, dtype=jnp.int32)
    places = (
        jnp.remainder(slot_ids // per_device - first_tile, axis_count)
        + slot_ids % per_device * axis_count
    )
    slot_valid = places < span_tiles
    return (slot_valid, jnp.where(slot_valid, places, 0))


def body(matrix, factors, starts):
    row_count = lax.axis_size("row")
    col_count = lax.axis_size("col")
    row_place = lax.axis_index("row")
    col_place = lax.axis_index("col")
    row_cycles = matrix.shape[0]
    tile_size = matrix.shape[2]
    col_cycles = matrix.shape[3]
    span_tiles = (WIN + SHIFT * (WINS - 1)) // tile_size
    first_tile = starts[0] // tile_size
    all_factors = lax.all_gather(factors, "col", axis=2, tiled=True)

    def left_step(window, band_rows):
        offset_row = starts[window] - starts[0]
        factor_now = lax.dynamic_index_in_dim(all_factors, window, 0, keepdims=False)
        window_rows = lax.dynamic_slice_in_dim(band_rows, offset_row, WIN, 0)
        result_rows = jnp.dot(
            factor_now.T,
            window_rows,
            precision=lax.Precision.HIGHEST,
            preferred_element_type=jnp.float32,
        )
        return lax.dynamic_update_slice_in_dim(band_rows, result_rows, offset_row, 0)

    def right_step(window, band_cols):
        offset_col = starts[window] - starts[0]
        factor_now = lax.dynamic_index_in_dim(all_factors, window, 0, keepdims=False)
        window_cols = lax.dynamic_slice_in_dim(band_cols, offset_col, WIN, 1)
        result_cols = jnp.dot(
            window_cols,
            factor_now,
            precision=lax.Precision.HIGHEST,
            preferred_element_type=jnp.float32,
        )
        return lax.dynamic_update_slice_in_dim(band_cols, result_cols, offset_col, 1)

    local_tiles = matrix.reshape(row_cycles, tile_size, col_cycles * tile_size)
    rows_each = -(-span_tiles // row_count)
    row_valid, row_index = pick_tiles(first_tile, rows_each, row_count, row_place, span_tiles)
    picked = jnp.where(row_valid[:, None, None], jnp.take(local_tiles, row_index, axis=0), 0.0)
    received = lax.all_to_all(picked, "row", split_axis=2, concat_axis=0, tiled=True)
    band_rows = jnp.take(received, band_order(first_tile, row_count, rows_each, span_tiles), axis=0)
    band_rows = band_rows.reshape(span_tiles * tile_size, received.shape[2])
    band_rows = lax.fori_loop(0, WINS, left_step, band_rows)
    row_tiles = band_rows.reshape(span_tiles, tile_size, received.shape[2])
    send_valid, send_place = slot_order(first_tile, row_count, rows_each, span_tiles)
    backsend = jnp.where(send_valid[:, None, None], jnp.take(row_tiles, send_place, axis=0), 0.0)
    returned = lax.all_to_all(backsend, "row", split_axis=0, concat_axis=2, tiled=True)
    for member in range(rows_each):
        local_tiles = jnp.where(
            row_valid[member],
            lax.dynamic_update_index_in_dim(local_tiles, returned[member], row_index[member], 0),
            local_tiles,
        )
    local_rows = row_cycles * tile_size
    column_view = local_tiles.reshape(local_rows, col_cycles, tile_size)
    cols_each = -(-span_tiles // col_count)
    col_valid, col_index = pick_tiles(first_tile, cols_each, col_count, col_place, span_tiles)
    picked_cols = jnp.where(col_valid[None, :, None], jnp.take(column_view, col_index, axis=1), 0.0)
    col_order = band_order(first_tile, col_count, cols_each, span_tiles)
    received_cols = lax.all_to_all(picked_cols, "col", split_axis=0, concat_axis=1, tiled=True)
    share_rows = received_cols.shape[0]
    band_cols = jnp.take(received_cols, col_order, axis=1).reshape(
        share_rows, span_tiles * tile_size
    )
    band_cols = lax.fori_loop(0, WINS, right_step, band_cols)
    slot_valid, slot_place = slot_order(first_tile, col_count, cols_each, span_tiles)
    send_cols = jnp.where(
        slot_valid[None, :, None],
        jnp.take(band_cols.reshape(share_rows, span_tiles, tile_size), slot_place, axis=1),
        0.0,
    )
    returned_cols = lax.all_to_all(send_cols, "col", split_axis=1, concat_axis=0, tiled=True)
    for member in range(cols_each):
        column_view = jnp.where(
            col_valid[member],
            lax.dynamic_update_index_in_dim(
                column_view, returned_cols[:, member], col_index[member], 1
            ),
            column_view,
        )
    return column_view.reshape(matrix.shape)


def solution(mesh):
    placed = (P(None, "row", None, None, "col", None), P(None, None, "col"), P())
    return jax.shard_map(
        body,
        mesh=mesh,
        in_specs=placed,
        out_specs=P(None, "row", None, None, "col", None),
        check_vma=False,
    )
```

profile of v0, /device:TPU:4, one launch (start us, length us, event | category | flops | bytes accessed | tf_op | source)
XLA Modules:
  0.0 2668.2 jit_solution(13656926926000482717)
XLA Ops:
  9.7 133.3 %reduce.3 = f32[6,128,128,128]{3,2,1,0:T(8,128)} reduce(f32[6,1,128,128,1,128]{5,4,3,2,1,0:T(1,128)} %param.7, f32[]{:T(128)} %broadcast.1276), dimensions={1,4}, to_apply=%param.7.reduce_sub_computation.3 | reduce | bytes 100663296 | tf_op args[0]
  143.0 53.6 %reshape.633 = f32[6,128,16384]{2,1,0:T(8,128)} reshape(f32[6,128,128,128]{3,2,1,0:T(8,128)} %reduce.3) | data formatting | bytes 100663296 | tf_op jit(solution)/shard_map/reshape | solution.py:72
  273.7 34.3 %fusion.10 = f32[6,128,16384]{2,1,0:T(8,128)} fusion(f32[6,128,5376]{2,1,0:T(8,128)} %gather_fusion.7, f32[6,128,5504]{2,1,0:T(8,128)} %gather_fusion.6, f32[6,128,5504]{2,1,0:T(8,128)} %gather_fusion.5, pred[6]{0:T(512)(128)(4,1)S(1)} %get-tuple-element.199, pred[6]{0:T(512)(128)(4,1)S(1)} %get-tuple-element.236), kind=kLoop, calls=%fused_computation.19 | loop fusion | flops 50331648 | bytes 100663312 | tf_op jit(solution)/shard_map/jit(_where)/select_n | solution.py:75
  308.0 58.4 %copy.74 = f32[6,128,16384]{1,0,2:T(8,128)} copy(f32[6,128,16384]{2,1,0:T(8,128)} %fusion.10) | data formatting | bytes 100663296 | tf_op jit(solution)/shard_map/jit(_where)/select_n | solution.py:75
  380.9 102.0 %all-gather.2.cloned.1.call-done = f32[10,512,512]{1,2,0:T(8,128)} async-done(((f32[10,512,64]{1,2,0:T(8,128)}), f32[10,512,512]{1,2,0:T(8,128)}) %all-gather.2.cloned.1.call-update) | async-done | bytes 10485776 | tf_op jit(solution)/shard_map/all_gather | solution.py:46
  494.1 606.8 %all-to-all-done = f32[6,128,16384]{1,0,2:T(8,128)} async-done(((f32[6,128,16384]{1,0,2:T(8,128)}), f32[6,128,16384]{1,0,2:T(8,128)}, u32[]{:S(2)}, u32[]{:S(2)}) %all-to-all-start) | async-done | bytes 50331680 | tf_op jit(solution)/shard_map/all_to_all | solution.py:76
  1100.9 58.1 %copy.76 = f32[4,6,128,4096]{3,2,1,0:T(8,128)} copy(f32[4,6,128,4096]{2,1,3,0:T(8,128)} %bitcast.10) | data formatting | bytes 100663296 | tf_op jit(solution)/shard_map/all_to_all | solution.py:76
  1159.0 32.2 %gather_fusion = f32[22,128,4096]{2,1,0:T(8,128)} fusion(f32[24,128,4096]{2,1,0:T(8,128)} %bitcast.115, s32[1024]{0:T(1024)S(1)} %pad_clamp_fusion.4), kind=kCustom, calls=%fused_computation | custom fusion | bytes 92274776 | tf_op jit(solution)/shard_map/jit(_take)/gather | solution.py:77
  1191.3 34.3 %bitcast_select_fusion = f32[2816,4096]{1,0:T(8,128)} fusion(f32[22,128,4096]{2,1,0:T(8,128)} %gather_fusion, pred[2816]{0:T(1024)(128)(4,1)S(1)} %broadcast_bitcast_fusion.1), kind=kLoop, calls=%fused_computation.21 | loop fusion | flops 11534336 | bytes 92277504 | tf_op jit(solution)/shard_map/jit(_take)/select_n | solution.py:77
  1225.5 415.1 %while.26 = (s32[]{:T(128)}, f32[2816,4096]{1,0:T(8,128)}, f32[10,512,512]{2,1,0:T(8,128)}, s32[10]{0:T(128)S(1)}, s32[]{:T(128)}, /*index=5*/s32[]{:T(128)}, s32[]{:T(128)}) while((s32[]{:T(128)}, f32[2816,4096]{1,0:T(8,128)}, f32[10,512,512]{2,1,0:T(8,128)}, s32[10]{0:T(128)S(1)}, s32[]{:T(128)}, /*index=5*/s32[]{:T(128)}, s32[]{:T(128)}) %tuple.96), condition=%wide.region_1.2_spmd, body=%wide.region_0.1_spmd.sunk | while | flops 12884901888 | bytes 34603672 | solution.py:79
  1244.8 22.3 dynamic_update_slice.27
  1286.4 22.3 dynamic_update_slice.27
  1369.5 22.3 dynamic_update_slice.27
  1452.7 22.3 dynamic_update_slice.27
  1535.8 22.3 dynamic_update_slice.27
  1640.7 33.7 %gather_fusion.1 = f32[24,128,4096]{2,1,0:T(8,128)} fusion(f32[22,128,4096]{2,1,0:T(8,128)} %bitcast.111, s32[1024]{0:T(1024)S(1)} %pad_clamp_fusion.3), kind=kCustom, calls=%fused_computation.1 | custom fusion | bytes 100663392 | tf_op jit(solution)/shard_map/jit(_take)/gather | solution.py:82
  1674.3 35.7 %select_select_fusion = f32[24,128,4096]{2,1,0:T(8,128)} fusion(f32[24,128,4096]{2,1,0:T(8,128)} %gather_fusion.1, pred[24]{0:T(512)(128)(4,1)S(1)} %copy-done.8, pred[24]{0:T(512)(128)(4,1)S(1)} %copy-done.9), kind=kLoop, calls=%fused_computation.20 | loop fusion | flops 25165824 | bytes 100663344 | tf_op jit(solution)/shard_map/jit(_where)/select_n | solution.py:82
  1736.7 527.0 %all-to-all-done.1 = f32[24,128,4096]{2,1,0:T(8,128)} async-done(((f32[24,128,4096]{2,1,0:T(8,128)}), f32[24,128,4096]{2,1,0:T(8,128)}, u32[]{:S(2)}, u32[]{:S(2)}) %all-to-all-start.1) | async-done | bytes 50331680 | tf_op jit(solution)/shard_map/all_to_all | solution.py:83
  2263.7 33.1 %slice_bitcast_fusion = (f32[4,1,16,8,4096]{4,3,2,1,0:T(8,128)}, f32[4,1,16,8,4096]{4,3,2,1,0:T(8,128)}, f32[4,1,16,8,4096]{4,3,2,1,0:T(8,128)}, f32[4,1,16,8,40...) fusion(f32[6,128,4,4096]{3,1,0,2:T(8,128)} %bitcast.17), kind=kLoop, calls=%fused_computation.22 | loop fusion | bytes 100663296
  2394.5 41.3 %copy.102 = f32[96,8,128,128]{3,2,1,0:T(8,128)} copy(f32[96,8,128,128]{3,1,2,0:T(8,128)} %bitcast.110) | data formatting | bytes 100663296
  2435.7 46.1 %copy.84 = f32[768,128,128]{2,0,1:T(8,128)} copy(f32[768,128,128]{2,1,0:T(8,128)} %bitcast.112) | data formatting | bytes 100663296 | tf_op jit(solution)/shard_map/reshape | solution.py:91
  2491.3 37.6 %all-to-all-done.2 = f32[768,3,128]{2,1,0:T(4,128)S(1)} async-done(((f32[768,3,128]{2,1,0:T(4,128)}), f32[768,3,128]{2,1,0:T(4,128)S(1)}, u32[]{:S(2)}, u32[]{:S(2)}) %all-to-all-start.2) | async-done | bytes 1179680 | tf_op jit(solution)/shard_map/all_to_all | solution.py:96
  2529.8 52.1 %while.27 = (s32[]{:T(128)}, f32[96,2816]{1,0:T(8,128)S(1)}, s32[10]{0:T(128)S(1)}, f32[10,512,512]{2,1,0:T(8,128)}, s32[]{:T(128)}, /*index=5*/s32[]{:T(128)}, s32[]{:T(128)}) while((s32[]{:T(128)}, f32[96,2816]{1,0:T(8,128)S(1)}, s32[10]{0:T(128)S(1)}, f32[10,512,512]{2,1,0:T(8,128)}, s32[]{:T(128)}, /*index=5*/s32[]{:T(128)}, ...), condition=%wide.region_3.4_spmd, body=%wide.region_2.3_spmd.sunk | while | flops 301989888 | bytes 1835671 | solution.py:101
  2594.2 22.6 all-to-all-done.3
  (166 shorter events, 608.6 us)
Async XLA Ops:
  230.7 43.1 %copy-start.2 = (pred[6]{0:T(512)(128)(4,1)}, pred[6]{0:T(512)(128)(4,1)S(1)}, u32[]{:S(2)}) copy-start(pred[6]{0:T(512)(128)(4,1)S(1)} %get-tuple-element.236) | copy-start | bytes 22
  366.4 734.6 %all-to-all-start = ((f32[6,128,16384]{1,0,2:T(8,128)}), f32[6,128,16384]{1,0,2:T(8,128)}, u32[]{:S(2)}, u32[]{:S(2)}) async-start(f32[6,128,16384]{1,0,2:T(8,128)} %copy.74), calls=%async_computation | async-start | bytes 134217728 | tf_op jit(solution)/shard_map/all_to_all | solution.py:76
  379.4 103.5 %all-gather.2.cloned.1.call-start = ((), (), s32[]{:S(2)}) async-start(), calls=%async_computation.4 | async-start | bytes 11796480 | tf_op jit(solution)/shard_map/all_gather | solution.py:46
  1191.3 34.3 %copy-start = (s32[10]{0:T(128)S(1)}, s32[10]{0:T(128)}, u32[]{:S(2)}) copy-start(s32[10]{0:T(128)} %param.9) | copy-start | bytes 124
  1640.7 33.7 %copy-start.8 = (pred[24]{0:T(512)(128)(4,1)S(1)}, pred[24]{0:T(512)(128)(4,1)}, u32[]{:S(2)}) copy-start(pred[24]{0:T(512)(128)(4,1)} %get-tuple-element.233) | copy-start | bytes 76
  1640.7 33.7 %copy-start.9 = (pred[24]{0:T(512)(128)(4,1)S(1)}, pred[24]{0:T(512)(128)(4,1)}, u32[]{:S(2)}) copy-start(pred[24]{0:T(512)(128)(4,1)} %get-tuple-element.234) | copy-start | bytes 76
  1710.0 12.8 copy-start.4
  1710.0 26.0 copy-start.3
  1710.0 553.6 %all-to-all-start.1 = ((f32[24,128,4096]{2,1,0:T(8,128)}), f32[24,128,4096]{2,1,0:T(8,128)}, u32[]{:S(2)}, u32[]{:S(2)}) async-start(f32[24,128,4096]{2,1,0:T(8,128)} %select_select_fusion), calls=%async_computation.1 | async-start | bytes 100663296 | tf_op jit(solution)/shard_map/all_to_all | solution.py:83
  2296.8 7.8 slice-start.8
  2296.8 7.8 slice-start.9
  2304.6 4.8 slice-start.6
  2304.6 6.5 slice-start.7
  2309.4 6.0 slice-start.4
  2311.1 4.6 slice-start.5
  2315.4 5.1 slice-start.2
  2315.7 6.2 slice-start.3
  2320.5 5.6 slice-start
  2435.7 48.2 %copy-start.5 = (pred[3]{0:T(512)(128)(4,1)S(1)}, pred[3]{0:T(512)(128)(4,1)}, u32[]{:S(2)}) copy-start(pred[3]{0:T(512)(128)(4,1)} %get-tuple-element.235) | copy-start | bytes 13
  2435.7 48.2 %copy-start.7 = (pred[3]{0:T(512)(128)(4,1)S(1)}, pred[3]{0:T(512)(128)(4,1)}, u32[]{:S(2)}) copy-start(pred[3]{0:T(512)(128)(4,1)} %get-tuple-element.197) | copy-start | bytes 13
  2481.9 47.9 %copy-start.1 = (s32[10]{0:T(128)S(1)}, s32[10]{0:T(128)}, u32[]{:S(2)}) copy-start(s32[10]{0:T(128)} %param.9) | copy-start | bytes 124
  2486.2 42.7 %all-to-all-start.2 = ((f32[768,3,128]{2,1,0:T(4,128)}), f32[768,3,128]{2,1,0:T(4,128)S(1)}, u32[]{:S(2)}, u32[]{:S(2)}) async-start(f32[768,3,128]{2,1,0:T(4,128)} %copy.85), calls=%async_computation.2 | async-start | bytes 3145728 | tf_op jit(solution)/shard_map/all_to_all | solution.py:96
  2529.7 57.8 %copy-start.6 = (s32[3]{0:T(128)S(1)}, s32[3]{0:T(128)}, u32[]{:S(2)}) copy-start(s32[3]{0:T(128)} %get-tuple-element.198) | copy-start | bytes 40
  2583.9 32.9 %all-to-all-start.3 = ((f32[96,24,128]{2,0,1:T(8,128)}), f32[96,24,128]{2,0,1:T(8,128)S(1)}, u32[]{:S(2)}, u32[]{:S(2)}) async-start(f32[96,24,128]{2,0,1:T(8,128)} %select_bitcast_fusion), calls=%async_computation.3 | async-start | bytes 2359296 | tf_op jit(solution)/shard_map/all_to_all | solution.py:108
  (1 other events, 4.5 us)
Sparse Core Ops, SparseCore 0:
  381.8 100.9 all-gather.1
where the time goes:
time: 2690 us; the launch traced here: 2670 us
  waiting for transfers between devices  1300 us (48%)
  local copies, waits for them, and re-layouts  770 us (29%)
  other arithmetic  315 us (12%)
  matrix products  194 us (7%)
  starting transfers between devices  34.5 us (1%)
  between operations  33.5 us (1%)
    all_to_all x1, waiting for transfers between devices, body(): lax.all_to_all(picked, 'row', split_axis=2, concat_axis=0, tiled=True)  607 us
    all_to_all x1, waiting for transfers between devices, body(): lax.all_to_all(backsend, 'row', split_axis=0, concat_axis=2, tiled=True)  527 us
    dynamic_update_slice x10, local copies, waits for them, and re-layouts, left_step(): lax.dynamic_update_slice_in_dim(band_rows, result_rows, offset_row, 0)  222 us
    dot_general x10, matrix products, left_step(): jnp.dot(factor_now.T, window_rows, precision=lax.Precision.HIGHEST, prefe...  174 us
    unnamed x6, other arithmetic  133 us
    all_gather x1, waiting for transfers between devices, body(): all_factors = lax.all_gather(factors, 'col', axis=2, tiled=True)  102 us
    unnamed x43, local copies, waits for them, and re-layouts  78.5 us
    gather x5, local copies, waits for them, and re-layouts, body(): jnp.take(local_tiles, row_index, axis=0)  76.6 us
  transfers between devices with their start and end apart: 5, of which 5 were waited for; matrix products, arithmetic and copies ran while one was open for 1% of the time, Pallas kernels for 0%

commit v1 on v0

v1 whole, which is shorter than its diff:
```python
import functools

import jax
import jax.numpy as jnp
from jax import lax
from jax.experimental import pallas as pl
from jax.experimental.pallas import tpu as pltpu
from jax.sharding import PartitionSpec as P

SHIFT = 256
CHUNKS = 4
GROUP = 2


def split(values):
    high = values.astype(jnp.bfloat16)
    low = (values - high.astype(jnp.float32)).astype(jnp.bfloat16)
    return high, low


def prepare_kernel(gathered, high_ref, low_ref):
    parts, each = gathered.shape[0], gathered.shape[2]
    for part in range(parts):
        high, low = split(gathered[part, 0])
        high_ref[0, pl.ds(part * each, each), :] = high
        low_ref[0, pl.ds(part * each, each), :] = low


def prepare(gathered):
    parts, wins, each, win = gathered.shape
    shape = jax.ShapeDtypeStruct((wins, win, win), jnp.bfloat16)
    spec = pl.BlockSpec((1, win, win), lambda w: (w, 0, 0))
    return pl.pallas_call(
        prepare_kernel,
        grid=(wins,),
        in_specs=[pl.BlockSpec((parts, 1, each, win), lambda w: (0, w, 0, 0))],
        out_specs=[spec, spec],
        out_shape=[shape, shape],
        name="prepare",
    )(gathered)


def left_kernel(peers, scalars, high_ref, low_ref, *refs):
    pieces, outs = refs[:peers], refs[peers : 2 * peers]
    band, done, in_sem, out_sem = refs[2 * peers :]
    cycles, tile, span, lanes = pieces[0].shape
    group = band.shape[2] // lanes
    steps = span // group
    wins, win, _ = high_ref.shape
    step = pl.program_id(0)
    slot = lax.rem(step, 2)
    me, first = scalars[0], scalars[1]

    def move(at, buffer, sem, into, begin):
        where = lax.rem(at, 2)
        if not begin:
            pltpu.make_async_copy(buffer.at[where], buffer.at[where], sem.at[where]).wait()
            return
        for offset in range(peers):
            source = jnp.bitwise_xor(me, offset)
            for cycle in range(cycles):
                row = pl.multiple_of((cycle * peers + source) * tile, tile)
                for lane in range(group):
                    near = buffer.at[where, pl.ds(row, tile), pl.ds(lane * lanes, lanes)]
                    if into:
                        far = pieces[offset].at[cycle, :, at * group + lane, :]
                        pltpu.make_async_copy(far, near, sem.at[where]).start()
                    else:
                        far = outs[offset].at[cycle, :, at * group + lane, :]
                        pltpu.make_async_copy(near, far, sem.at[where]).start()

    @pl.when(step == 0)
    def _():
        move(step, band, in_sem, True, True)

    @pl.when(step + 1 < steps)
    def _():
        move(step + 1, band, in_sem, True, True)

    @pl.when(step >= 2)
    def _():
        move(step - 2, done, out_sem, False, False)

    move(step, band, in_sem, True, False)
    start = pl.multiple_of(first * tile, tile)
    total = band.shape[1]
    shift = SHIFT
    covered = win + shift * (wins - 1)
    if total > covered:
        done[slot, pl.ds(0, total - covered), :] = band[slot, pl.ds(0, total - covered), :]
        done[slot, pl.ds(covered, total - covered), :] = band[slot, pl.ds(covered, total - covered), :]

    def window(w, _):
        top = pl.multiple_of(start + w * shift, tile)
        rows = pl.ds(top, win)
        x_high, x_low = split(band[slot, rows, :])
        factor = high_ref[w]
        y = jnp.dot(factor, x_high, preferred_element_type=jnp.float32)
        y += jnp.dot(factor, x_low, preferred_element_type=jnp.float32)
        y += jnp.dot(low_ref[w], x_high, preferred_element_type=jnp.float32)
        done[slot, pl.ds(top, shift), :] = y[:shift]
        band[slot, pl.ds(pl.multiple_of(top + shift, tile), win - shift), :] = y[shift:]
        return 0

    lax.fori_loop(0, wins, window, 0)
    last = pl.ds(pl.multiple_of(start + wins * shift, tile), win - shift)
    done[slot, last, :] = band[slot, last, :]
    move(step, done, out_sem, False, True)

    @pl.when(step == steps - 1)
    def _():
        if steps > 1:
            move(step - 1, done, out_sem, False, False)
        move(step, done, out_sem, False, False)


def left(scalars, high, low, pieces):
    peers = len(pieces)
    cycles, tile, span, lanes = pieces[0].shape
    group = GROUP if span % GROUP == 0 else 1
    rows = cycles * peers * tile
    wins, win, _ = high.shape
    whole = pl.BlockSpec(memory_space=pl.ANY)
    resident = pl.BlockSpec((wins, win, win), lambda g, s: (0, 0, 0), pipeline_mode=pl.Buffered(1))
    cols = span * lanes
    return pl.pallas_call(
        functools.partial(left_kernel, peers),
        grid_spec=pltpu.PrefetchScalarGridSpec(
            num_scalar_prefetch=1,
            grid=(span // group,),
            in_specs=[resident, resident] + [whole] * peers,
            out_specs=[whole] * peers,
            scratch_shapes=[
                pltpu.VMEM((2, rows, group * lanes), jnp.float32),
                pltpu.VMEM((2, rows, group * lanes), jnp.float32),
                pltpu.SemaphoreType.DMA((2,)),
                pltpu.SemaphoreType.DMA((2,)),
            ],
        ),
        out_shape=[jax.ShapeDtypeStruct(p.shape, p.dtype) for p in pieces],
        compiler_params=pltpu.CompilerParams(
            dimension_semantics=("arbitrary",), vmem_limit_bytes=48 << 20
        ),
        cost_estimate=pl.CostEstimate(
            flops=6 * wins * win * win * cols,
            bytes_accessed=8 * rows * cols + 4 * wins * win * win,
            transcendentals=0,
        ),
        name="left",
    )(scalars, high, low, *pieces)


def right_kernel(scalars, high_ref, low_ref, picked, out, band):
    parts, cycles, rows, lanes = picked.shape
    wins, win, _ = high_ref.shape
    shift = SHIFT
    for part in range(parts):
        for cycle in range(cycles):
            band[cycle * parts + part] = picked[part, cycle]
    first = scalars[1]
    tiles, pace = win // lanes, shift // lanes

    def window(w, _):
        top = first + w * pace
        x = jnp.concatenate([band[top + t] for t in range(tiles)], axis=1)
        x_high, x_low = split(x)
        dims = (((1,), (1,)), ((), ()))
        y = lax.dot_general(x_high, high_ref[w], dims, preferred_element_type=jnp.float32)
        y += lax.dot_general(x_low, high_ref[w], dims, preferred_element_type=jnp.float32)
        y += lax.dot_general(x_high, low_ref[w], dims, preferred_element_type=jnp.float32)
        for t in range(tiles):
            band[top + t] = y[:, t * lanes : (t + 1) * lanes]
        return 0

    lax.fori_loop(0, wins, window, 0)
    for part in range(parts):
        for cycle in range(cycles):
            out[part, cycle] = band[cycle * parts + part]


def right(scalars, high, low, picked):
    parts, cycles, rows, lanes = picked.shape
    wins, win, _ = high.shape
    vmem = pl.BlockSpec(memory_space=pltpu.VMEM)
    return pl.pallas_call(
        right_kernel,
        in_specs=[pl.BlockSpec(memory_space=pltpu.SMEM), vmem, vmem, vmem],
        out_specs=vmem,
        out_shape=jax.ShapeDtypeStruct(picked.shape, picked.dtype),
        scratch_shapes=[pltpu.VMEM((parts * cycles, rows, lanes), jnp.float32)],
        compiler_params=pltpu.CompilerParams(vmem_limit_bytes=40 << 20),
        cost_estimate=pl.CostEstimate(
            flops=6 * wins * win * win * rows,
            bytes_accessed=8 * picked.size + 4 * wins * win * win,
            transcendentals=0,
        ),
        name="right",
    )(scalars, high, low, picked)


def body(matrix, factors, starts):
    peers = lax.axis_size("row")
    parts = lax.axis_size("col")
    me = lax.axis_index("row")
    place = lax.axis_index("col")
    cycles, _, tile, width, _, lanes = matrix.shape
    first = starts[0] // tile
    scalars = jnp.stack([me.astype(jnp.int32), first.astype(jnp.int32)])
    each = width // peers
    chunks = CHUNKS if each % (8 * CHUNKS) == 0 else 1
    span = each // chunks
    near = -(-cycles * peers // parts)
    tiles = matrix.reshape(cycles, tile, peers, chunks, span, lanes)

    turned = jnp.swapaxes(factors, 1, 2)
    gathered = lax.all_gather(turned, "col", axis=0)
    high, low = prepare(gathered)

    head = tiles[:, :, 0, 0]
    rows = cycles * tile // parts
    front = head[:, :, :near].reshape(parts, rows, near, lanes)
    front = jnp.swapaxes(front, 1, 2)
    front = lax.all_to_all(front, "col", split_axis=0, concat_axis=0, tiled=True)
    front = right(scalars, high, low, front)
    front = lax.all_to_all(front, "col", split_axis=0, concat_axis=0, tiled=True)
    front = jnp.swapaxes(front, 1, 2).reshape(cycles, tile, near, lanes)
    head = jnp.concatenate([front, head[:, :, near:]], axis=2)

    def piece(owner, chunk):
        value = lax.dynamic_index_in_dim(tiles, owner, 2, keepdims=False)[:, :, chunk]
        if chunk == 0:
            value = jnp.where(owner == 0, head, value)
        return value

    def swap(value, offset):
        return lax.ppermute(value, "row", [(i, i ^ offset) for i in range(peers)])

    order = list(range(1, chunks)) + [0]
    result = tiles
    for chunk in order:
        pieces = [piece(me, chunk)]
        pieces += [swap(piece(jnp.bitwise_xor(me, offset), chunk), offset) for offset in range(1, peers)]
        pieces = left(scalars, high, low, pieces)
        for offset in range(peers):
            value = pieces[offset] if offset == 0 else swap(pieces[offset], offset)
            owner = jnp.bitwise_xor(me, offset)
            result = lax.dynamic_update_slice(
                result, value[:, :, None, None], (0, 0, owner, chunk, 0, 0)
            )
    return result.reshape(matrix.shape)


def solution(mesh):
    placed = (P(None, "row", None, None, "col", None), P(None, None, "col"), P())
    return jax.shard_map(
        body,
        mesh=mesh,
        in_specs=placed,
        out_specs=P(None, "row", None, None, "col", None),
        check_vma=False,
    )
```

time: 2690 us -> 1190 us (0.44)
  local copies, waits for them, and re-layouts: 770 us -> 184 us
  waiting for transfers between devices: 1300 us -> 778 us
  other arithmetic: 315 us -> 9.87 us
  matrix products: 194 us -> 0 us
  Pallas kernels: 0 us -> 158 us
    all_to_all x4 -> x2, waiting for transfers between devices: 1190 us -> 7.11 us  [body(): lax.all_to_all(front, 'col', split_axis=0, concat_axis=0, tiled=True)]
    ppermute x0 -> x24, waiting for transfers between devices: none -> 768 us  [swap(): return lax.ppermute(value, 'row', [(i, i ^ offset) for i in range(peers)])]
    dynamic_update_slice x20 -> x15, local copies, waits for them, and re-layouts: 236 us -> 41.4 us  [body(): lax.dynamic_update_slice(result, value[:, :, None, None], (0, 0, owner, c...]
    dot_general x20 -> x0, matrix products: 194 us -> none  [the longest x10 174 us: left_step(): jnp.dot(factor_now.T, window_rows, precision=lax.Precision.HIGHEST, prefe...]
    select_n x21 -> x1, other arithmetic: 179 us -> 9.79 us  [piece(): value = jnp.where(owner == 0, head, value)]
    pallas_call x0 -> x6, Pallas kernels: none -> 158 us  [the longest x4 139 us: left(): pl.pallas_call(functools.partial(left_kernel, peers), grid_spec=pltpu.Pre...]
    gather x10 -> x0, local copies, waits for them, and re-layouts: 146 us -> none  [the longest x5 76.6 us: body(): jnp.take(local_tiles, row_index, axis=0)]
    unnamed x6 -> x0, other arithmetic: 133 us -> none
  transfers between devices with their start and end apart: 5 -> 27, of which waited for: 5 -> 18; matrix products, arithmetic and copies ran while one was open for 1% -> 12% of each run, Pallas kernels for 0% -> 13%
where the time goes in v1:
time: 1190 us; the launch traced here: 1180 us
  waiting for transfers between devices  778 us (65%)
  local copies, waits for them, and re-layouts  184 us (15%)
  Pallas kernels  158 us (13%)
  starting transfers between devices  41.3 us (3%)
  between operations  13.7 us (1%)
    ppermute x24, waiting for transfers between devices, swap(): return lax.ppermute(value, 'row', [(i, i ^ offset) for i in range(peers)])  768 us
    pallas_call x4, Pallas kernels, left(): pl.pallas_call(functools.partial(left_kernel, peers), grid_spec=pltpu.Pre...  139 us
    squeeze x6, local copies, waits for them, and re-layouts, piece(): lax.dynamic_index_in_dim(tiles, owner, 2, keepdims=False)[:, :, chunk]  51.8 us
    unnamed x17, local copies, waits for them, and re-layouts  45.7 us
    dynamic_update_slice x15, local copies, waits for them, and re-layouts, body(): lax.dynamic_update_slice(result, value[:, :, None, None], (0, 0, owner, c...  41.4 us
    dynamic_slice x1, local copies, waits for them, and re-layouts, piece(): lax.dynamic_index_in_dim(tiles, owner, 2, keepdims=False)[:, :, chunk]  33.4 us
    ppermute x24, starting transfers between devices, swap(): return lax.ppermute(value, 'row', [(i, i ^ offset) for i in range(peers)])  32 us
  transfers between devices with their start and end apart: 27, of which 18 were waited for; matrix products, arithmetic and copies ran while one was open for 12% of the time, Pallas kernels for 13%

profile of v1, /device:TPU:4, one launch (start us, length us, event | category | flops | bytes accessed | tf_op | source)
XLA Modules:
  0.0 1184.8 jit_solution(13914581648265464963)
XLA Ops:
  6.5 33.2 %copy.78 = f32[6,1,128,128,1,128]{5,4,3,2,1,0:T(1,128)} copy(f32[6,1,128,128,1,128]{5,4,3,2,1,0:T(1,128)} %param.3) | data formatting | bytes 100663296
  39.8 33.4 %constant_dynamic-slice_fusion = (f32[6,128,1,4,8,128]{5,4,3,2,1,0:T(8,128)}, f32[6,128,1,4,8,128]{5,4,3,2,1,0:T(8,128)}, f32[6,128,1,4,8,128]{5,4,3,2,1,0:T(8,128)}, f32[6,128,1,4,8,128]{5,4,3,2,1,0:T(8,128)}) fusion(f32[6,128,4,4,8,128]{5,4,3,2,1,0:T(8,128)} %bitcast.132, s32[]{:T(128)S(6)} %select_n.76, s32[]{:T(128)S(6)} %select_n.75, s32[]{:T(128)S(6)} %select_n.74, ...), kind=kLoop, calls=%fused_computation.43 | loop fusion | bytes 100663312 | tf_op jit(solution)/shard_map/jit(dynamic_index_in_dim)/dynamic_slice | solution.py:230
  73.2 14.2 %copy_bitcast_fusion = (f32[6,128,4,8,128]{4,3,1,0,2:T(8,128)S(1)}, f32[6,128,4,8,128]{4,3,1,0,2:T(8,128)}) fusion(f32[6,128,1,4,8,128]{5,4,3,2,1,0:T(8,128)} %get-tuple-element.43, f32[6,128,1,4,8,128]{5,4,3,2,1,0:T(8,128)} %get-tuple-element.44), kind=kLoop, calls=%fused_computation | loop fusion | bytes 50331648 | tf_op jit(solution)/shard_map/jit(dynamic_index_in_dim)/squeeze | solution.py:230
  104.5 14.3 %copy_bitcast_fusion.2 = (f32[6,128,4,8,128]{4,3,1,0,2:T(8,128)S(1)}, f32[6,128,4,8,128]{4,3,1,0,2:T(8,128)}) fusion(f32[6,128,1,4,8,128]{5,4,3,2,1,0:T(8,128)} %get-tuple-element.45, f32[6,128,1,4,8,128]{5,4,3,2,1,0:T(8,128)} %get-tuple-element.46), kind=kLoop, calls=%fused_computation.2 | loop fusion | bytes 50331648 | tf_op jit(solution)/shard_map/jit(dynamic_index_in_dim)/squeeze | solution.py:230
  151.8 14.0 %collective-permute-done.2.refs_3_ = f32[6,128,8,128]{3,2,1,0:T(8,128)} collective-permute-done((f32[6,128,8,128]{3,2,1,0:T(8,128)S(1)}, f32[6,128,8,128]{3,2,1,0:T(8,128)}, u32[]{:S(2)}, u32[]{:S(2)}) %collective-permute-start.2) | collective-permute-done | bytes 3145760 | tf_op jit(solution)/shard_map/ppermute | solution.py:236
  167.3 66.0 %collective-permute-done.1.refs_2_ = f32[6,128,8,128]{3,2,1,0:T(8,128)} collective-permute-done((f32[6,128,8,128]{3,2,1,0:T(8,128)}, f32[6,128,8,128]{3,2,1,0:T(8,128)}, u32[]{:S(2)}, u32[]{:S(2)}) %collective-permute-start.1) | collective-permute-done | bytes 3145760 | tf_op jit(solution)/shard_map/ppermute | solution.py:236
  233.3 34.8 %left.4 = (f32[6,128,8,128]{3,2,1,0:T(8,128)S(1)}, f32[6,128,8,128]{3,2,1,0:T(8,128)}, f32[6,128,8,128]{3,2,1,0:T(8,128)}, f32[6,128,8,128]{3,2,1,0:T(8,128)}) custom-call(s32[2]{0:T(128)S(1)} %pad_add_fusion.scalars, bf16[10,512,512]{2,1,0:T(8,128)(2,1)} %get-tuple-element.23.high_ref, bf16[10,512,512]{2,1,0:T(8,128)(2,1)} %get-tuple-element.24.low_ref, ...), custom_call_target="tpu_custom_call" | custom-call | flops 16106127360 | bytes 35651584 | tf_op jit(solution)/shard_map/left/pallas_call | solution.py:126
  282.8 17.8 %collective-permute-done.8.refs_3_ = f32[6,128,8,128]{3,2,1,0:T(8,128)} collective-permute-done((f32[6,128,8,128]{3,2,1,0:T(8,128)}, f32[6,128,8,128]{3,2,1,0:T(8,128)}, u32[]{:S(2)}, u32[]{:S(2)}) %collective-permute-start.8) | collective-permute-done | bytes 3145760 | tf_op jit(solution)/shard_map/ppermute | solution.py:236
  326.5 41.6 %collective-permute-done.7.refs_2_ = f32[6,128,8,128]{3,2,1,0:T(8,128)} collective-permute-done((f32[6,128,8,128]{3,2,1,0:T(8,128)}, f32[6,128,8,128]{3,2,1,0:T(8,128)}, u32[]{:S(2)}, u32[]{:S(2)}) %collective-permute-start.7) | collective-permute-done | bytes 3145760 | tf_op jit(solution)/shard_map/ppermute | solution.py:236
  370.1 34.8 %left.5 = (f32[6,128,8,128]{3,2,1,0:T(8,128)S(1)}, f32[6,128,8,128]{3,2,1,0:T(8,128)}, f32[6,128,8,128]{3,2,1,0:T(8,128)}, f32[6,128,8,128]{3,2,1,0:T(8,128)}) custom-call(s32[2]{0:T(128)S(1)} %pad_add_fusion.scalars, bf16[10,512,512]{2,1,0:T(8,128)(2,1)} %get-tuple-element.23.high_ref, bf16[10,512,512]{2,1,0:T(8,128)(2,1)} %get-tuple-element.24.low_ref, ...), custom_call_target="tpu_custom_call" | custom-call | flops 16106127360 | bytes 35651584 | tf_op jit(solution)/shard_map/left/pallas_call | solution.py:126
  404.8 30.7 %collective-permute-done.14.refs_3_ = f32[6,128,8,128]{3,2,1,0:T(8,128)} collective-permute-done((f32[6,128,8,128]{3,2,1,0:T(8,128)}, f32[6,128,8,128]{3,2,1,0:T(8,128)}, u32[]{:S(2)}, u32[]{:S(2)}) %collective-permute-start.14) | collective-permute-done | bytes 3145760 | tf_op jit(solution)/shard_map/ppermute | solution.py:236
  437.0 64.8 %collective-permute-done.13.refs_2_ = f32[6,128,8,128]{3,2,1,0:T(8,128)} collective-permute-done((f32[6,128,8,128]{3,2,1,0:T(8,128)}, f32[6,128,8,128]{3,2,1,0:T(8,128)}, u32[]{:S(2)}, u32[]{:S(2)}) %collective-permute-start.13) | collective-permute-done | bytes 3145760 | tf_op jit(solution)/shard_map/ppermute | solution.py:236
  519.3 49.6 %collective-permute-done.3 = f32[6,128,8,128]{3,2,1,0:T(8,128)} collective-permute-done((f32[6,128,8,128]{3,2,1,0:T(8,128)}, f32[6,128,8,128]{3,2,1,0:T(8,128)}, u32[]{:S(2)}, u32[]{:S(2)}) %collective-permute-start.3) | collective-permute-done | bytes 3145760 | tf_op jit(solution)/shard_map/ppermute | solution.py:236
  572.4 65.4 %collective-permute-done.5 = f32[6,128,8,128]{3,2,1,0:T(8,128)} collective-permute-done((f32[6,128,8,128]{3,2,1,0:T(8,128)}, f32[6,128,8,128]{3,2,1,0:T(8,128)}, u32[]{:S(2)}, u32[]{:S(2)}) %collective-permute-start.5) | collective-permute-done | bytes 3145760 | tf_op jit(solution)/shard_map/ppermute | solution.py:236
  637.8 65.9 %collective-permute-done.9 = f32[6,128,8,128]{3,2,1,0:T(8,128)} collective-permute-done((f32[6,128,8,128]{3,2,1,0:T(8,128)}, f32[6,128,8,128]{3,2,1,0:T(8,128)}, u32[]{:S(2)}, u32[]{:S(2)}) %collective-permute-start.9) | collective-permute-done | bytes 3145760 | tf_op jit(solution)/shard_map/ppermute | solution.py:236
  706.7 34.8 %left.6 = (f32[6,128,8,128]{3,2,1,0:T(8,128)S(1)}, f32[6,128,8,128]{3,2,1,0:T(8,128)}, f32[6,128,8,128]{3,2,1,0:T(8,128)}, f32[6,128,8,128]{3,2,1,0:T(8,128)}) custom-call(s32[2]{0:T(128)S(1)} %pad_add_fusion.scalars, bf16[10,512,512]{2,1,0:T(8,128)(2,1)} %get-tuple-element.23.high_ref, bf16[10,512,512]{2,1,0:T(8,128)(2,1)} %get-tuple-element.24.low_ref, ...), custom_call_target="tpu_custom_call" | custom-call | flops 16106127360 | bytes 35651584 | tf_op jit(solution)/shard_map/left/pallas_call | solution.py:126
  741.5 31.2 %collective-permute-done.20.refs_3_ = f32[6,128,8,128]{3,2,1,0:T(8,128)} collective-permute-done((f32[6,128,8,128]{3,2,1,0:T(8,128)}, f32[6,128,8,128]{3,2,1,0:T(8,128)}, u32[]{:S(2)}, u32[]{:S(2)}) %collective-permute-start.20) | collective-permute-done | bytes 3145760 | tf_op jit(solution)/shard_map/ppermute | solution.py:236
  785.4 53.2 %collective-permute-done.18.refs_1_ = f32[6,128,8,128]{3,2,1,0:T(8,128)} collective-permute-done((f32[6,128,8,128]{3,2,1,0:T(8,128)}, f32[6,128,8,128]{3,2,1,0:T(8,128)}, u32[]{:S(2)}, u32[]{:S(2)}) %collective-permute-start.18) | collective-permute-done | bytes 3145760 | tf_op jit(solution)/shard_map/ppermute | solution.py:236
  842.1 34.7 %left.7 = (f32[6,128,8,128]{3,2,1,0:T(8,128)S(1)}, f32[6,128,8,128]{3,2,1,0:T(8,128)}, f32[6,128,8,128]{3,2,1,0:T(8,128)}, f32[6,128,8,128]{3,2,1,0:T(8,128)}) custom-call(s32[2]{0:T(128)S(1)} %pad_add_fusion.scalars, bf16[10,512,512]{2,1,0:T(8,128)(2,1)} %get-tuple-element.23.high_ref, bf16[10,512,512]{2,1,0:T(8,128)(2,1)} %get-tuple-element.24.low_ref, ...), custom_call_target="tpu_custom_call" | custom-call | flops 16106127360 | bytes 35651584 | tf_op jit(solution)/shard_map/left/pallas_call | solution.py:126
  878.8 28.6 %collective-permute-done.11 = f32[6,128,8,128]{3,2,1,0:T(8,128)S(1)} collective-permute-done((f32[6,128,8,128]{3,2,1,0:T(8,128)}, f32[6,128,8,128]{3,2,1,0:T(8,128)S(1)}, u32[]{:S(2)}, u32[]{:S(2)}) %collective-permute-start.11) | collective-permute-done | bytes 3145760 | tf_op jit(solution)/shard_map/ppermute | solution.py:236
  911.4 62.1 %collective-permute-done.15 = f32[6,128,8,128]{3,2,1,0:T(8,128)} collective-permute-done((f32[6,128,8,128]{3,2,1,0:T(8,128)}, f32[6,128,8,128]{3,2,1,0:T(8,128)}, u32[]{:S(2)}, u32[]{:S(2)}) %collective-permute-start.15) | collective-permute-done | bytes 3145760 | tf_op jit(solution)/shard_map/ppermute | solution.py:236
  989.6 52.9 %collective-permute-done.17 = f32[6,128,8,128]{3,2,1,0:T(8,128)} collective-permute-done((f32[6,128,8,128]{3,2,1,0:T(8,128)}, f32[6,128,8,128]{3,2,1,0:T(8,128)}, u32[]{:S(2)}, u32[]{:S(2)}) %collective-permute-start.17) | collective-permute-done | bytes 3145760 | tf_op jit(solution)/shard_map/ppermute | solution.py:236
  1048.1 60.2 %collective-permute-done.21 = f32[6,128,8,128]{3,2,1,0:T(8,128)S(1)} collective-permute-done((f32[6,128,8,128]{3,2,1,0:T(8,128)}, f32[6,128,8,128]{3,2,1,0:T(8,128)S(1)}, u32[]{:S(2)}, u32[]{:S(2)}) %collective-permute-start.21) | collective-permute-done | bytes 3145760 | tf_op jit(solution)/shard_map/ppermute | solution.py:236
  1112.0 64.0 %collective-permute-done.23 = f32[6,128,8,128]{3,2,1,0:T(8,128)S(1)} collective-permute-done((f32[6,128,8,128]{3,2,1,0:T(8,128)S(1)}, f32[6,128,8,128]{3,2,1,0:T(8,128)S(1)}, u32[]{:S(2)}, u32[]{:S(2)}) %collective-permute-start.23) | collective-permute-done | bytes 3145760 | tf_op jit(solution)/shard_map/ppermute | solution.py:236
  (83 shorter events, 168.7 us)
Async XLA Ops:
  6.5 133.9 %all-gather.3.cloned.1.call-start = ((), (), s32[]{:S(2)}) async-start(), calls=%async_computation.2 | async-start | bytes 11796480 | tf_op jit(solution)/shard_map/all_gather | solution.py:216
  102.9 130.4 %collective-permute-start.1 = (f32[6,128,8,128]{3,2,1,0:T(8,128)}, f32[6,128,8,128]{3,2,1,0:T(8,128)}, u32[]{:S(2)}, u32[]{:S(2)}) collective-permute-start(f32[6,128,8,128]{3,2,1,0:T(8,128)} %get-tuple-element.52), channel_id=1, source_target_pairs={{0,16},{8,24},{16,0},{24,8},{1,17},{9,25},{17,1},{25,9},{2,18},{10... | collective-permute-start | bytes 9437192 | tf_op jit(solution)/shard_map/ppermute | solution.py:236
  126.7 173.9 %collective-permute-start.8 = (f32[6,128,8,128]{3,2,1,0:T(8,128)}, f32[6,128,8,128]{3,2,1,0:T(8,128)}, u32[]{:S(2)}, u32[]{:S(2)}) collective-permute-start(f32[6,128,8,128]{3,2,1,0:T(8,128)} %get-tuple-element.48), channel_id=1, source_target_pairs={{0,24},{8,16},{16,8},{24,0},{1,25},{9,17},{17,9},{25,1},{2,26},{10... | collective-permute-start | bytes 9437192 | tf_op jit(solution)/shard_map/ppermute | solution.py:236
  128.2 239.9 %collective-permute-start.7 = (f32[6,128,8,128]{3,2,1,0:T(8,128)}, f32[6,128,8,128]{3,2,1,0:T(8,128)}, u32[]{:S(2)}, u32[]{:S(2)}) collective-permute-start(f32[6,128,8,128]{3,2,1,0:T(8,128)} %get-tuple-element.51), channel_id=1, source_target_pairs={{0,16},{8,24},{16,0},{24,8},{1,17},{9,25},{17,1},{25,9},{2,18},{10... | collective-permute-start | bytes 9437192 | tf_op jit(solution)/shard_map/ppermute | solution.py:236
  165.8 203.8 %collective-permute-start.6 = (f32[6,128,8,128]{3,2,1,0:T(8,128)}, f32[6,128,8,128]{3,2,1,0:T(8,128)}, u32[]{:S(2)}, u32[]{:S(2)}) collective-permute-start(f32[6,128,8,128]{3,2,1,0:T(8,128)} %get-tuple-element.54), channel_id=1, source_target_pairs={{0,8},{8,0},{16,24},{24,16},{1,9},{9,1},{17,25},{25,17},{2,10},{10... | collective-permute-start | bytes 9437192 | tf_op jit(solution)/shard_map/ppermute | solution.py:236
  279.9 155.6 %collective-permute-start.14 = (f32[6,128,8,128]{3,2,1,0:T(8,128)}, f32[6,128,8,128]{3,2,1,0:T(8,128)}, u32[]{:S(2)}, u32[]{:S(2)}) collective-permute-start(f32[6,128,8,128]{3,2,1,0:T(8,128)} %get-tuple-element.47), channel_id=1, source_target_pairs={{0,24},{8,16},{16,8},{24,0},{1,25},{9,17},{17,9},{25,1},{2,26},{10... | collective-permute-start | bytes 9437192 | tf_op jit(solution)/shard_map/ppermute | solution.py:236
  281.3 220.5 %collective-permute-start.13 = (f32[6,128,8,128]{3,2,1,0:T(8,128)}, f32[6,128,8,128]{3,2,1,0:T(8,128)}, u32[]{:S(2)}, u32[]{:S(2)}) collective-permute-start(f32[6,128,8,128]{3,2,1,0:T(8,128)} %get-tuple-element.50), channel_id=1, source_target_pairs={{0,16},{8,24},{16,0},{24,8},{1,17},{9,25},{17,1},{25,9},{2,18},{10... | collective-permute-start | bytes 9437192 | tf_op jit(solution)/shard_map/ppermute | solution.py:236
  300.7 218.3 %collective-permute-start.12 = (f32[6,128,8,128]{3,2,1,0:T(8,128)}, f32[6,128,8,128]{3,2,1,0:T(8,128)}, u32[]{:S(2)}, u32[]{:S(2)}) collective-permute-start(f32[6,128,8,128]{3,2,1,0:T(8,128)} %get-tuple-element.53), channel_id=1, source_target_pairs={{0,8},{8,0},{16,24},{24,16},{1,9},{9,1},{17,25},{25,17},{2,10},{10... | collective-permute-start | bytes 9437192 | tf_op jit(solution)/shard_map/ppermute | solution.py:236
  322.1 185.0 %all-to-all-start.1 = ((f32[8,3,96,128]{3,2,1,0:T(8,128)}), f32[8,3,96,128]{3,2,1,0:T(8,128)}, u32[]{:S(2)}, u32[]{:S(2)}) async-start(f32[8,3,96,128]{3,2,1,0:T(8,128)} %right.1), calls=%async_computation.1 | async-start | bytes 2359296 | tf_op jit(solution)/shard_map/all_to_all | solution.py:225
  368.1 200.8 %collective-permute-start.3 = (f32[6,128,8,128]{3,2,1,0:T(8,128)}, f32[6,128,8,128]{3,2,1,0:T(8,128)}, u32[]{:S(2)}, u32[]{:S(2)}) collective-permute-start(f32[6,128,8,128]{3,2,1,0:T(8,128)} %get-tuple-element.26), channel_id=1, source_target_pairs={{0,8},{8,0},{16,24},{24,16},{1,9},{9,1},{17,25},{25,17},{2,10},{10... | collective-permute-start | bytes 9437192 | tf_op jit(solution)/shard_map/ppermute | solution.py:236
  369.6 201.3 %collective-permute-start.4 = (f32[6,128,8,128]{3,2,1,0:T(8,128)}, f32[6,128,8,128]{3,2,1,0:T(8,128)}, u32[]{:S(2)}, u32[]{:S(2)}) collective-permute-start(f32[6,128,8,128]{3,2,1,0:T(8,128)} %get-tuple-element.27), channel_id=1, source_target_pairs={{0,16},{8,24},{16,0},{24,8},{1,17},{9,25},{17,1},{25,9},{2,18},{10... | collective-permute-start | bytes 9437192 | tf_op jit(solution)/shard_map/ppermute | solution.py:236
  435.5 202.3 %collective-permute-start.5 = (f32[6,128,8,128]{3,2,1,0:T(8,128)}, f32[6,128,8,128]{3,2,1,0:T(8,128)}, u32[]{:S(2)}, u32[]{:S(2)}) collective-permute-start(f32[6,128,8,128]{3,2,1,0:T(8,128)} %get-tuple-element.28), channel_id=1, source_target_pairs={{0,24},{8,16},{16,8},{24,0},{1,25},{9,17},{17,9},{25,1},{2,26},{10... | collective-permute-start | bytes 9437192 | tf_op jit(solution)/shard_map/ppermute | solution.py:236
  501.8 202.0 %collective-permute-start.9 = (f32[6,128,8,128]{3,2,1,0:T(8,128)}, f32[6,128,8,128]{3,2,1,0:T(8,128)}, u32[]{:S(2)}, u32[]{:S(2)}) collective-permute-start(f32[6,128,8,128]{3,2,1,0:T(8,128)} %get-tuple-element.30), channel_id=1, source_target_pairs={{0,8},{8,0},{16,24},{24,16},{1,9},{9,1},{17,25},{25,17},{2,10},{10... | collective-permute-start | bytes 9437192 | tf_op jit(solution)/shard_map/ppermute | solution.py:236
  519.0 253.7 %collective-permute-start.20 = (f32[6,128,8,128]{3,2,1,0:T(8,128)}, f32[6,128,8,128]{3,2,1,0:T(8,128)}, u32[]{:S(2)}, u32[]{:S(2)}) collective-permute-start(f32[6,128,8,128]{3,2,1,0:T(8,128)} %get-tuple-element.59), channel_id=1, source_target_pairs={{0,24},{8,16},{16,8},{24,0},{1,25},{9,17},{17,9},{25,1},{2,26},{10... | collective-permute-start | bytes 9437192 | tf_op jit(solution)/shard_map/ppermute | solution.py:236
  568.9 269.7 %collective-permute-start.18 = (f32[6,128,8,128]{3,2,1,0:T(8,128)}, f32[6,128,8,128]{3,2,1,0:T(8,128)}, u32[]{:S(2)}, u32[]{:S(2)}) collective-permute-start(f32[6,128,8,128]{3,2,1,0:T(8,128)} %get-tuple-element.60), channel_id=1, source_target_pairs={{0,8},{8,0},{16,24},{24,16},{1,9},{9,1},{17,25},{25,17},{2,10},{10... | collective-permute-start | bytes 9437192 | tf_op jit(solution)/shard_map/ppermute | solution.py:236
  570.9 269.8 %collective-permute-start.19 = (f32[6,128,8,128]{3,2,1,0:T(8,128)S(1)}, f32[6,128,8,128]{3,2,1,0:T(8,128)}, u32[]{:S(2)}, u32[]{:S(2)}) collective-permute-start(f32[6,128,8,128]{3,2,1,0:T(8,128)S(1)} %get-tuple-element.61), channel_id=1, source_target_pairs={{0,16},{8,24},{16,0},{24,8},{1,17},{9,25},{17,1},{25,9},{2,18},{10... | collective-permute-start | bytes 9437192 | tf_op jit(solution)/shard_map/ppermute | solution.py:236
  637.8 239.0 %collective-permute-start.10 = (f32[6,128,8,128]{3,2,1,0:T(8,128)}, f32[6,128,8,128]{3,2,1,0:T(8,128)S(1)}, u32[]{:S(2)}, u32[]{:S(2)}) collective-permute-start(f32[6,128,8,128]{3,2,1,0:T(8,128)} %get-tuple-element.31), channel_id=1, source_target_pairs={{0,16},{8,24},{16,0},{24,8},{1,17},{9,25},{17,1},{25,9},{2,18},{10... | collective-permute-start | bytes 9437192 | tf_op jit(solution)/shard_map/ppermute | solution.py:236
  703.8 203.7 %collective-permute-start.11 = (f32[6,128,8,128]{3,2,1,0:T(8,128)}, f32[6,128,8,128]{3,2,1,0:T(8,128)S(1)}, u32[]{:S(2)}, u32[]{:S(2)}) collective-permute-start(f32[6,128,8,128]{3,2,1,0:T(8,128)} %get-tuple-element.32), channel_id=1, source_target_pairs={{0,24},{8,16},{16,8},{24,0},{1,25},{9,17},{17,9},{25,1},{2,26},{10... | collective-permute-start | bytes 9437192 | tf_op jit(solution)/shard_map/ppermute | solution.py:236
  772.7 200.8 %collective-permute-start.15 = (f32[6,128,8,128]{3,2,1,0:T(8,128)}, f32[6,128,8,128]{3,2,1,0:T(8,128)}, u32[]{:S(2)}, u32[]{:S(2)}) collective-permute-start(f32[6,128,8,128]{3,2,1,0:T(8,128)} %get-tuple-element.34), channel_id=1, source_target_pairs={{0,8},{8,0},{16,24},{24,16},{1,9},{9,1},{17,25},{25,17},{2,10},{10... | collective-permute-start | bytes 9437192 | tf_op jit(solution)/shard_map/ppermute | solution.py:236
  838.7 147.2 %collective-permute-start.16 = (f32[6,128,8,128]{3,2,1,0:T(8,128)}, f32[6,128,8,128]{3,2,1,0:T(8,128)}, u32[]{:S(2)}, u32[]{:S(2)}) collective-permute-start(f32[6,128,8,128]{3,2,1,0:T(8,128)} %get-tuple-element.35), channel_id=1, source_target_pairs={{0,16},{8,24},{16,0},{24,8},{1,17},{9,25},{17,1},{25,9},{2,18},{10... | collective-permute-start | bytes 9437192 | tf_op jit(solution)/shard_map/ppermute | solution.py:236
  840.7 201.8 %collective-permute-start.17 = (f32[6,128,8,128]{3,2,1,0:T(8,128)}, f32[6,128,8,128]{3,2,1,0:T(8,128)}, u32[]{:S(2)}, u32[]{:S(2)}) collective-permute-start(f32[6,128,8,128]{3,2,1,0:T(8,128)} %get-tuple-element.36), channel_id=1, source_target_pairs={{0,24},{8,16},{16,8},{24,0},{1,25},{9,17},{17,9},{25,1},{2,26},{10... | collective-permute-start | bytes 9437192 | tf_op jit(solution)/shard_map/ppermute | solution.py:236
  876.8 231.5 %collective-permute-start.21 = (f32[6,128,8,128]{3,2,1,0:T(8,128)}, f32[6,128,8,128]{3,2,1,0:T(8,128)S(1)}, u32[]{:S(2)}, u32[]{:S(2)}) collective-permute-start(f32[6,128,8,128]{3,2,1,0:T(8,128)} %get-tuple-element.38), channel_id=1, source_target_pairs={{0,8},{8,0},{16,24},{24,16},{1,9},{9,1},{17,25},{25,17},{2,10},{10... | collective-permute-start | bytes 9437192 | tf_op jit(solution)/shard_map/ppermute | solution.py:236
  907.5 202.7 %collective-permute-start.22 = (f32[6,128,8,128]{3,2,1,0:T(8,128)S(1)}, f32[6,128,8,128]{3,2,1,0:T(8,128)S(1)}, u32[]{:S(2)}, u32[]{:S(2)}) collective-permute-start(f32[6,128,8,128]{3,2,1,0:T(8,128)S(1)} %copy-done.7), channel_id=1, source_target_pairs={{0,16},{8,24},{16,0},{24,8},{1,17},{9,25},{17,1},{25,9},{2,18},{10... | collective-permute-start | bytes 9437192 | tf_op jit(solution)/shard_map/ppermute | solution.py:236
  973.5 202.5 %collective-permute-start.23 = (f32[6,128,8,128]{3,2,1,0:T(8,128)S(1)}, f32[6,128,8,128]{3,2,1,0:T(8,128)S(1)}, u32[]{:S(2)}, u32[]{:S(2)}) collective-permute-start(f32[6,128,8,128]{3,2,1,0:T(8,128)S(1)} %copy-done.6), channel_id=1, source_target_pairs={{0,24},{8,16},{16,8},{24,0},{1,25},{9,17},{17,9},{25,1},{2,26},{10... | collective-permute-start | bytes 9437192 | tf_op jit(solution)/shard_map/ppermute | solution.py:236
  (11 other events, 341.3 us)
Sparse Core Ops, SparseCore 0:
  39.8 100.5 all-gather.2
